TPU v7x, 32 devices: a whole 2x2x4 slice. The times are simulated.
32 devices in a mesh: grp: 2 (over x), yz: 8 (over z, y), gx: 2 (over core).
Axes of the slice: x: 2, y: 2, z: 4, core: 2. Of those that a mesh axis runs over, the one named last changes fastest.
Arguments:
- field: bfloat16 [4096, 256, 128], P(('grp', 'gx'), 'yz'), parts along dimension 0, may hold values from -6 to 6
- sketch_seeds: int32 [12], P('grp'), parts along dimension 0, may hold values from 1 to 32748
Outputs:
- basis: float32 [4096, 256], P(('grp', 'gx')), parts along dimension 0
- core: bfloat16 [512, 256, 128], P(('grp', 'gx'), 'yz'), parts along dimension 0
There are 2 independent parts, one for each index of `grp`. A program takes and returns all parts, laid end to end along the dimension named above; each array names one. Nothing has to cross between parts.
All inputs are finite; a program needn't handle non-finite values.
Results may differ from a plain program's by a relative error of at most 0.0057.
Values sent between devices are 32-bit elements; how exact they have to be, the bound alone decides.
No kernel may reach another device: no remote copies, remote signals or barrier semaphores. Data moves between devices by JAX's collectives and lax.ppermute only.
A program may use at most 64 MiB of HBM per device.

v0:
```python
import math
import jax
import jax.numpy as jnp
from jax import lax
from jax.sharding import PartitionSpec as P

RANK = 256
prime = 32749


def omega_table(seeds, start, count):
    place = (start + jnp.arange(count, dtype=jnp.int32) + 1)[:, None]
    column = (jnp.arange(RANK, dtype=jnp.int32) + 1)[None, :]
    first = seeds[0] * place % prime
    second = (seeds[1] * column + seeds[2]) % prime
    square = place * place % prime
    third = seeds[2] * column % prime
    mixed = (first * second % prime + square * third % prime) % prime
    return mixed.astype(jnp.float32) * (2.0 / prime) - 1.0


def local(field, sketch_seeds):
    x_local, y_local, z_local = field.shape
    y_start = lax.axis_index("yz") * y_local
    omega_z = omega_table(sketch_seeds[3:6], 0, z_local).astype(jnp.bfloat16)
    omega_y = omega_table(sketch_seeds[0:3], y_start, y_local)
    block = math.gcd(y_local, 8)

    def add_block(total, index):
        rows = lax.dynamic_slice_in_dim(field, index * block, block, 1)
        proj = jnp.dot(
            rows.reshape(x_local * block, z_local), omega_z, preferred_element_type=jnp.float32
        ).reshape(x_local, block, RANK)
        weight_y = lax.dynamic_slice_in_dim(omega_y, index * block, block, 0)
        return (total + jnp.sum(proj * weight_y[None], axis=1), None)

    partial_value, unused = lax.scan(
        add_block,
        jnp.zeros((x_local, RANK), jnp.float32),
        jnp.arange(y_local // block, dtype=jnp.int32),
    )
    sketch = lax.psum(partial_value, "yz")
    gram = lax.psum(
        jnp.dot(
            sketch.T, sketch, precision=lax.Precision.HIGHEST, preferred_element_type=jnp.float32
        ),
        "gx",
    )
    lower = jnp.linalg.cholesky(gram)
    basis = lax.linalg.triangular_solve(
        lower, sketch, left_side=False, lower=True, transpose_a=True
    )
    basis_half = basis.astype(jnp.bfloat16)
    flat = field.reshape(x_local, y_local * z_local)
    owned_rank = RANK // lax.axis_size("gx")
    core = lax.psum_scatter(
        lax.dot_general(
            basis_half, flat, (((0,), (0,)), ((), ())), preferred_element_type=jnp.float32
        ),
        "gx",
        scatter_dimension=0,
        tiled=True,
    )
    return (basis, core.reshape(owned_rank, y_local, z_local).astype(jnp.bfloat16))


def solution(mesh):
    in_specs = (P(("grp", "gx"), "yz", None), P("grp"))
    out_specs = (P(("grp", "gx"), None), P(("grp", "gx"), "yz", None))
    return jax.shard_map(local, mesh=mesh, in_specs=in_specs, out_specs=out_specs, check_vma=False)
```

profile of v0, /device:TPU:0, one launch (start us, length us, event | category | flops | bytes accessed | tf_op | source)
XLA Modules:
  0.0 233.7 jit_solution(5224184737601147460)
XLA Ops:
  7.2 1.6 fusion.53
  10.1 1.3 and_select_fusion.4
  11.4 1.2 and_select_fusion
  12.8 20.5 %while.13 = (s32[]{:T(128)}, f32[1024,256]{1,0:T(8,128)S(1)}, s32[4]{0:T(128)S(1)}, bf16[1024,32,128]{2,1,0:T(8,128)(2,1)}, f32[32,256]{1,0:T(8,128)S(1)}, /*ind...) while((s32[]{:T(128)}, f32[1024,256]{1,0:T(8,128)S(1)}, ...), condition=%wide.region_2.3_spmd.clone, body=%wide.region_0.2_spmd.clone.sunk | while | flops 542146560 | bytes 10513617 | solution.py:37
  14.1 1.7 constant_dynamic-slice_fusion.8
  15.9 1.7 multiply_reduce_fusion.2
  19.3 1.7 constant_dynamic-slice_fusion.8
  21.0 1.7 multiply_reduce_fusion.2
  24.4 1.7 constant_dynamic-slice_fusion.8
  26.1 1.7 multiply_reduce_fusion.2
  29.5 1.7 constant_dynamic-slice_fusion.8
  31.3 1.7 multiply_reduce_fusion.2
  33.3 1.0 copy-done
  34.3 81.1 %all-reduce.4.cloned.1.call-done = f32[1024,256]{1,0:T(8,128)} async-done(((f32[1024,256]{1,0:T(8,128)}), f32[1024,256]{1,0:T(8,128)}) %all-reduce.4.cloned.1.call-update) | async-done | bytes 1048592 | tf_op jit(solution)/shard_map/psum | solution.py:42
  115.4 4.1 %fusion.54 = f32[256,256]{0,1:T(8,128)} fusion(f32[1024,256]{1,0:T(8,128)} %all-reduce.4.cloned.1.call-done), kind=kOutput, calls=%fused_computation.98 | convolution fusion | flops 805306368 | bytes 1310720 | tf_op jit(solution)/shard_map/dot_general | solution.py:44
  119.8 17.7 %all-reduce.6.cloned.1.call-done = f32[256,256]{0,1:T(8,128)} async-done(((f32[256,256]{0,1:T(8,128)}), f32[256,256]{0,1:T(8,128)}) %all-reduce.6.cloned.1.call-update) | async-done | bytes 262160 | tf_op jit(solution)/shard_map/psum | solution.py:43
  137.6 1.1 copy.6
  138.6 1.0 fusion.35
  139.6 11.7 %cholesky.50 = f32[128,128]{1,0:T(8,128)S(1)} custom-call(f32[128,128]{1,0:T(8,128)S(1)} %cholesky.118), custom_call_target="Cholesky" | custom-call | tf_op jit(solution)/shard_map/jit(cholesky)/cholesky | solution.py:49
  152.0 9.8 %custom-call.14 = f32[1,128,128]{1,2,0:T(8,128)S(1)} custom-call(f32[1,128,128]{2,1,0:T(8,128)S(1)} %get-tuple-element.121), custom_call_target="InvertDiagBlocksLowerTriangular" | custom-call | tf_op jit(solution)/shard_map/jit(cholesky)/cholesky | solution.py:49
  162.4 11.7 %cholesky.105 = f32[128,128]{1,0:T(8,128)S(1)} custom-call(f32[128,128]{1,0:T(8,128)S(1)} %convolution_subtract_fusion.1), custom_call_target="Cholesky" | custom-call | tf_op jit(solution)/shard_map/jit(cholesky)/cholesky | solution.py:49
  174.1 0.7 compare_reduce_fusion
  176.3 4.3 %while.12 = (s32[]{:T(128)}, f32[256,256]{1,0:T(8,128)S(1)}, s32[2,2]{1,0:T(2,128)S(1)}, f32[2,128,128]{2,1,0:T(8,128)S(1)}, s32[]{:T(128)}) while((s32[]{:T(128)}, f32[256,256]{1,0:T(8,128)S(1)}, s32[2,2]{1,0:T(2,128)S(1)}, f32[2,128,128]{2,1,0:T(8,128)S(1)}, s32[]{:T(128)}) %tuple.57), condition=%wide.while_cond, body=%wide.while_body.sunk | while | flops 2 | bytes 131189 | solution.py:50
  177.1 1.4 bitcast_dynamic-update-slice_fusion.2
  179.1 1.4 bitcast_dynamic-update-slice_fusion.2
  180.5 19.7 %custom-call.15 = f32[2,128,128]{1,2,0:T(8,128)S(1)} custom-call(f32[2,128,128]{2,1,0:T(8,128)S(1)} %get-tuple-element.42), custom_call_target="InvertDiagBlocksLowerTriangular" | custom-call | tf_op jit(solution)/shard_map/triangular_solve | solution.py:50
  200.9 1.0 convolution_subtract_fusion
  202.5 8.3 %fusion.29 = f32[256,4096]{1,0:T(8,128)} fusion(bf16[128,8,32,128]{3,2,1,0:T(8,128)(2,1)} %bitcast.54, f32[1024,128]{0,1:T(8,128)S(1)} %fusion.36, f32[1024,128]{0,1:T(8,128)S(1)} %fusion.32), kind=kOutput, calls=%fused_computation.38 | convolution fusion | flops 2148532224 | bytes 13631488 | tf_op jit(solution)/shard_map/dot_general | solution.py:57
  210.9 1.3 copy.7
  212.2 12.0 %reduce-scatter.2.cloned.1.call-done = f32[128,4096]{1,0:T(8,128)} async-done(((f32[256,4096]{1,0:T(8,128)}), f32[128,4096]{1,0:T(8,128)}) %reduce-scatter.2.cloned.1.call-update) | async-done | bytes 2097168 | tf_op jit(solution)/shard_map/reduce_scatter | solution.py:56
  224.2 1.8 convert_bitcast_fusion
  226.0 1.2 copy.11
  (44 shorter events, 9.4 us)
Async XLA Ops:
  7.2 108.2 %all-reduce.4.cloned.1.call-start = ((), (), s32[]{:S(2)}) async-start(), calls=%async_computation.1 | async-start | bytes 2097152 | tf_op jit(solution)/shard_map/psum | solution.py:42
  33.3 1.0 copy-start
  34.3 103.3 %all-reduce.6.cloned.1.call-start = ((), (), s32[]{:S(2)}) async-start(), calls=%async_computation.2 | async-start | bytes 524288 | tf_op jit(solution)/shard_map/psum | solution.py:43
  115.4 84.8 %copy-start.1 = (f32[1024,256]{1,0:T(8,128)S(1)}, f32[1024,256]{1,0:T(8,128)}, u32[]{:S(2)}) copy-start(f32[1024,256]{1,0:T(8,128)} %all-reduce.4.cloned.1.call-done) | copy-start | bytes 3145732
  119.6 104.6 %reduce-scatter.2.cloned.1.call-start = ((), (), s32[]{:S(2)}) async-start(), calls=%async_computation.3 | async-start | bytes 6291456 | tf_op jit(solution)/shard_map/reduce_scatter | solution.py:56
Sparse Core Ops, SparseCore 0:
  34.4 80.9 all-reduce.3
  119.7 17.8 all-reduce.5
  210.9 13.2 reduce-scatter.1
where the time goes:
time: 234 us
  waiting for transfers between devices  111 us (47%)
  other arithmetic  62.3 us (27%)
  matrix products  21.9 us (9%)
  local copies, waits for them, and re-layouts  19.9 us (9%)
  between operations  15.3 us (7%)
  loops' own time  3.19 us (1%)
    psum x1, waiting for transfers between devices, local(): sketch = lax.psum(partial_value, 'yz')  81.1 us
    another operation x7, other arithmetic, local(): lower = jnp.linalg.cholesky(gram)  34.7 us
    another operation x4, other arithmetic, local(): lax.linalg.triangular_solve(lower, sketch, left_side=False, lower=True, t...  19.8 us
    psum x1, waiting for transfers between devices, local(): lax.psum(jnp.dot(sketch.T, sketch, precision=lax.Precision.HIGHEST, prefe...  17.7 us
    reduce_scatter x1, waiting for transfers between devices, local(): lax.psum_scatter(lax.dot_general(basis_half, flat, (((0,), (0,)), ((), ()...  12 us
    dot_general x1, matrix products, local(): lax.dot_general(basis_half, flat, (((0,), (0,)), ((), ())), preferred_ele...  8.29 us
    dynamic_slice x4, local copies, waits for them, and re-layouts, add_block(): rows = lax.dynamic_slice_in_dim(field, index * block, block, 1)  6.93 us
    dot_general x4, matrix products, add_block(): jnp.dot(rows.reshape(x_local * block, z_local), omega_z, preferred_elemen...  6.81 us
  transfers between devices with their start and end apart: 3, of which 3 were waited for; matrix products, arithmetic and copies ran while one was open for 1% of the time, Pallas kernels for 0%

commit v1 on v0

--- a/solution.py
+++ b/solution.py
@@ -40,11 +40,17 @@
         jnp.arange(y_local // block, dtype=jnp.int32),
     )
     sketch = lax.psum(partial_value, "yz")
-    gram = lax.psum(
-        jnp.dot(
-            sketch.T, sketch, precision=lax.Precision.HIGHEST, preferred_element_type=jnp.float32
+    gram = jnp.sum(
+        lax.all_gather(
+            jnp.dot(
+                sketch.T,
+                sketch,
+                precision=lax.Precision.HIGHEST,
+                preferred_element_type=jnp.float32,
+            ),
+            "gx",
         ),
-        "gx",
+        axis=0,
     )
     lower = jnp.linalg.cholesky(gram)
     basis = lax.linalg.triangular_solve(

time: 234 us -> 215 us (0.919)
  waiting for transfers between devices: 111 us -> 91.5 us
  blocking collectives: 0 us -> 2.36 us
    psum x1 -> x0, waiting for transfers between devices: 17.7 us -> none  [local(): lax.psum(jnp.dot(sketch.T, sketch, precision=lax.Precision.HIGHEST, prefe...]
    all_gather x0 -> x1, blocking collectives: none -> 2.36 us  [local(): lax.all_gather(jnp.dot(sketch.T, sketch, precision=lax.Precision.HIGHEST,...]
  transfers between devices with their start and end apart: 3 -> 2, of which waited for: 3 -> 2; matrix products, arithmetic and copies ran while one was open for 1% -> 1% of each run, Pallas kernels for 0% -> 0%
where the time goes in v1:
time: 215 us; the launch traced here: 214 us
  waiting for transfers between devices  91.5 us (43%)
  other arithmetic  61.3 us (29%)
  matrix products  21.3 us (10%)
  local copies, waits for them, and re-layouts  18.9 us (9%)
  between operations  15.6 us (7%)
  loops' own time  3.19 us (1%)
  blocking collectives  2.36 us (1%)
    psum x1, waiting for transfers between devices, local(): sketch = lax.psum(partial_value, 'yz')  81.1 us
    another operation x7, other arithmetic, local(): lower = jnp.linalg.cholesky(gram)  34.7 us
    another operation x4, other arithmetic, local(): lax.linalg.triangular_solve(lower, sketch, left_side=False, lower=True, t...  19.8 us
    reduce_scatter x1, waiting for transfers between devices, local(): lax.psum_scatter(lax.dot_general(basis_half, flat, (((0,), (0,)), ((), ()...  10.4 us
    dot_general x1, matrix products, local(): lax.dot_general(basis_half, flat, (((0,), (0,)), ((), ())), preferred_ele...  8.3 us
    dynamic_slice x4, local copies, waits for them, and re-layouts, add_block(): rows = lax.dynamic_slice_in_dim(field, index * block, block, 1)  6.93 us
    dot_general x4, matrix products, add_block(): jnp.dot(rows.reshape(x_local * block, z_local), omega_z, preferred_elemen...  6.81 us
  transfers between devices with their start and end apart: 2, of which 2 were waited for; matrix products, arithmetic and copies ran while one was open for 1% of the time, Pallas kernels for 0%

profile of v1, /device:TPU:0, one launch (start us, length us, event | category | flops | bytes accessed | tf_op | source)
XLA Modules:
  0.0 214.2 jit_solution(5610417340013014138)
XLA Ops:
  7.2 1.6 fusion.53
  8.8 0.7 and_select_fusion.5
  10.1 1.3 and_select_fusion.4
  11.4 1.2 and_select_fusion
  12.8 20.5 %while.13 = (s32[]{:T(128)}, f32[1024,256]{1,0:T(8,128)S(1)}, s32[4]{0:T(128)S(1)}, bf16[1024,32,128]{2,1,0:T(8,128)(2,1)}, f32[32,256]{1,0:T(8,128)S(1)}, /*ind...) while((s32[]{:T(128)}, f32[1024,256]{1,0:T(8,128)S(1)}, ...), condition=%wide.region_2.3_spmd.clone, body=%wide.region_0.2_spmd.clone.sunk | while | flops 542146560 | bytes 10513617 | solution.py:37
  12.8 0.7 dynamic_slice.20
  14.1 1.7 constant_dynamic-slice_fusion.8
  15.9 1.7 multiply_reduce_fusion.2
  19.3 1.7 constant_dynamic-slice_fusion.8
  21.0 1.7 multiply_reduce_fusion.2
  24.4 1.7 constant_dynamic-slice_fusion.8
  26.1 1.7 multiply_reduce_fusion.2
  29.5 1.7 constant_dynamic-slice_fusion.8
  31.3 1.7 multiply_reduce_fusion.2
  33.3 1.0 copy-done
  34.3 81.1 %all-reduce.3.cloned.1.call-done = f32[1024,256]{1,0:T(8,128)} async-done(((f32[1024,256]{1,0:T(8,128)}), f32[1024,256]{1,0:T(8,128)}) %all-reduce.3.cloned.1.call-update) | async-done | bytes 1048592 | tf_op jit(solution)/shard_map/psum | solution.py:42
  115.4 3.4 %fusion.54 = f32[256,256]{1,0:T(8,128)S(1)} fusion(f32[1024,256]{1,0:T(8,128)} %all-reduce.3.cloned.1.call-done), kind=kOutput, calls=%fused_computation.98 | convolution fusion | flops 805306368 | bytes 1310720 | tf_op jit(solution)/shard_map/dot_general | solution.py:45
  118.9 2.4 %all-gather = f32[512,256]{1,0:T(8,128)S(1)} all-gather(f32[256,256]{1,0:T(8,128)S(1)} %fusion.54), channel_id=2, replica_groups=mesh['grp'=2,'yz'=8,'gx'=2] {'gx'}, dimensions={0}, use_global_device_ids=true | all-gather | bytes 786432 | tf_op jit(solution)/shard_map/all_gather | solution.py:44
  121.5 11.7 %cholesky.50 = f32[128,128]{1,0:T(8,128)S(1)} custom-call(f32[128,128]{1,0:T(8,128)S(1)} %cholesky.118), custom_call_target="Cholesky" | custom-call | tf_op jit(solution)/shard_map/jit(cholesky)/cholesky | solution.py:55
  133.9 9.8 %custom-call.14 = f32[1,128,128]{1,2,0:T(8,128)S(1)} custom-call(f32[1,128,128]{2,1,0:T(8,128)S(1)} %get-tuple-element.132), custom_call_target="InvertDiagBlocksLowerTriangular" | custom-call | tf_op jit(solution)/shard_map/jit(cholesky)/cholesky | solution.py:55
  144.2 11.7 %cholesky.105 = f32[128,128]{1,0:T(8,128)S(1)} custom-call(f32[128,128]{1,0:T(8,128)S(1)} %convolution_subtract_fusion.1), custom_call_target="Cholesky" | custom-call | tf_op jit(solution)/shard_map/jit(cholesky)/cholesky | solution.py:55
  155.9 0.7 compare_reduce_fusion
  158.1 4.3 %while.12 = (s32[]{:T(128)}, f32[256,256]{1,0:T(8,128)S(1)}, s32[2,2]{1,0:T(2,128)S(1)}, f32[2,128,128]{2,1,0:T(8,128)S(1)}, s32[]{:T(128)}) while((s32[]{:T(128)}, f32[256,256]{1,0:T(8,128)S(1)}, s32[2,2]{1,0:T(2,128)S(1)}, f32[2,128,128]{2,1,0:T(8,128)S(1)}, s32[]{:T(128)}) %tuple.59), condition=%wide.while_cond, body=%wide.while_body.sunk | while | flops 2 | bytes 131189 | solution.py:56
  158.9 1.4 bitcast_dynamic-update-slice_fusion.2
  160.9 1.4 bitcast_dynamic-update-slice_fusion.2
  162.4 19.7 %custom-call.15 = f32[2,128,128]{1,2,0:T(8,128)S(1)} custom-call(f32[2,128,128]{2,1,0:T(8,128)S(1)} %get-tuple-element.42), custom_call_target="InvertDiagBlocksLowerTriangular" | custom-call | tf_op jit(solution)/shard_map/triangular_solve | solution.py:56
  182.7 1.0 convolution_subtract_fusion
  184.3 8.3 %fusion.29 = f32[256,4096]{1,0:T(8,128)} fusion(bf16[128,8,32,128]{3,2,1,0:T(8,128)(2,1)} %bitcast.55, f32[1024,128]{0,1:T(8,128)S(1)} %fusion.36, f32[1024,128]{0,1:T(8,128)S(1)} %fusion.32), kind=kOutput, calls=%fused_computation.38 | convolution fusion | flops 2148532224 | bytes 13631488 | tf_op jit(solution)/shard_map/dot_general | solution.py:63
  192.7 1.3 copy.9
  194.0 10.4 %reduce-scatter.2.cloned.1.call-done = f32[128,4096]{1,0:T(8,128)} async-done(((f32[256,4096]{1,0:T(8,128)}), f32[128,4096]{1,0:T(8,128)}) %reduce-scatter.2.cloned.1.call-update) | async-done | bytes 2097168 | tf_op jit(solution)/shard_map/reduce_scatter | solution.py:62
  204.4 1.8 convert_bitcast_fusion
  206.2 1.2 copy.12
  (43 shorter events, 8.0 us)
Async XLA Ops:
  7.2 108.2 %all-reduce.3.cloned.1.call-start = ((), (), s32[]{:S(2)}) async-start(), calls=%async_computation.1 | async-start | bytes 2097152 | tf_op jit(solution)/shard_map/psum | solution.py:42
  33.3 1.0 copy-start
  34.3 170.1 %reduce-scatter.2.cloned.1.call-start = ((), (), s32[]{:S(2)}) async-start(), calls=%async_computation.2 | async-start | bytes 6291456 | tf_op jit(solution)/shard_map/reduce_scatter | solution.py:62
  115.4 66.6 %copy-start.1 = (f32[1024,256]{1,0:T(8,128)S(1)}, f32[1024,256]{1,0:T(8,128)}, u32[]{:S(2)}) copy-start(f32[1024,256]{1,0:T(8,128)} %all-reduce.3.cloned.1.call-done) | copy-start | bytes 3145732
Sparse Core Ops, SparseCore 0:
  34.4 80.9 all-reduce.2
  192.7 11.6 reduce-scatter.1
